TPU v7x, 32 devices: a whole 2x2x4 slice. The times are simulated.
32 devices in a mesh: expert: 8 (over z, x), tensor: 4 (over y, core).
Axes of the slice: x: 2, y: 2, z: 4, core: 2. Of those that a mesh axis runs over, the one named last changes fastest.
Arguments:
- tokens: bfloat16 [4096, 1024], P('expert'), may hold values from -6 to 6
- teacher: bfloat16 [4096, 1024], P('expert'), may hold values from -6 to 6
- valid_mask: int32 [4096], P('expert'), may hold values from 0 to 1, as said below
- routes: int32 [4096, 8], P('expert'), may hold values from 0 to 31, all different within a row; in each aligned block of 512 rows (0 to 511, 512 to 1023, ...) at most 192 rows name the same one
- first_gain: float32 [1024], replicated, may hold values from 0.5 to 1.5
- query_weight: bfloat16 [1024, 1024], P(None, 'tensor'), may hold values from -0.75 to 0.75
- key_matrix: bfloat16 [1024, 512], P(None, 'tensor'), may hold values from -0.75 to 0.75
- value_matrix: bfloat16 [1024, 512], P(None, 'tensor'), may hold values from -0.1875 to 0.1875
- output_weight: bfloat16 [1024, 1024], P('tensor'), may hold values from -3 to 3
- second_gain: float32 [1024], replicated, may hold values from 0.5 to 1.5
- router_weight: bfloat16 [1024, 32], replicated, may hold values from -0.09375 to 0.09375
- expert_in: bfloat16 [64, 2, 512, 512], P('expert', None, None, 'tensor'), may hold values from -0.1875 to 0.1875
- expert_out: bfloat16 [64, 512, 512], P('expert', 'tensor'), may hold values from -3 to 3
Outputs:
- layer_output: bfloat16 [4096, 1024], P('expert')
- mean_loss: float32 [], replicated
- grad_tokens: float32 [4096, 1024], P('expert')
- grad_first_gain: float32 [1024], replicated
- grad_query: float32 [1024, 1024], P(None, 'tensor')
- grad_key: float32 [1024, 512], P(None, 'tensor')
- grad_value: float32 [1024, 512], P(None, 'tensor')
- grad_output: float32 [1024, 1024], P('tensor')
- grad_second_gain: float32 [1024], replicated
- grad_router: float32 [1024, 32], replicated
- grad_expert_in: float32 [64, 2, 512, 512], P('expert', None, None, 'tensor')
- grad_expert_out: float32 [64, 512, 512], P('expert', 'tensor')
Inputs may be any that keep to these rules, and one draw needn't show every extreme that they name: `routes`: each row names 8 different experts; among the 512 rows of one device no expert is named more than 192 times, a bound that some block reaches. `valid_mask`: the last of each device's 512 rows is 1.
All inputs are finite; a program needn't handle non-finite values.
Results may differ from a plain program's by a relative error of at most 0.017.
The roundings to bfloat16 on the way count: a program that leaves them out, or rounds other values in their place, can miss the bound.
Values may be sent and summed in bfloat16 or wider, within the bound.
No kernel may reach another device: no remote copies, remote signals or barrier semaphores. Data moves between devices by JAX's collectives and lax.ppermute only.
A program may use at most 192 MiB of HBM per device.

v0:
```python
import jax
import jax.numpy as jnp
from jax import lax
from jax.sharding import PartitionSpec as P

HEAD_DIM = 64
TOP = 8
BLOCK = 256
EPS = 1e-06
ATTN_SCALE = 0.015625
RESIDUAL = 0.22
THETA = 10000.0


def shifted(value, axis, steps):
    count = lax.axis_size(axis)
    pairs = [(source, (source + steps) % count) for source in range(count)]
    return lax.ppermute(value, axis, pairs)


def rope_tables(length, head_size):
    half_size = head_size // 2
    frequency = THETA ** (-(jnp.arange(half_size, dtype=jnp.float32) * 2.0) / head_size)
    angle_table = jnp.arange(length, dtype=jnp.float32)[:, None] * frequency[None, :]
    return (jnp.cos(angle_table)[:, None, :], jnp.sin(angle_table)[:, None, :])


def apply_rotary(values, cosine_lookup, sine_lookup):
    half_size = values.shape[-1] // 2
    lower_half, upper_half = (values[..., :half_size], values[..., half_size:])
    return jnp.concatenate(
        [
            lower_half * cosine_lookup - upper_half * sine_lookup,
            upper_half * cosine_lookup + lower_half * sine_lookup,
        ],
        -1,
    )


def unrotate(grads, cosine_lookup, sine_lookup):
    half_size = grads.shape[-1] // 2
    lower_half, upper_half = (grads[..., :half_size], grads[..., half_size:])
    return jnp.concatenate(
        [
            lower_half * cosine_lookup + upper_half * sine_lookup,
            upper_half * cosine_lookup - lower_half * sine_lookup,
        ],
        -1,
    )


def normalize(values):
    row_peak = jnp.max(values, -1, keepdims=True)
    exp_scores = jnp.exp(values - row_peak)
    return exp_scores / jnp.sum(exp_scores, -1, keepdims=True)


def slot_tables(route_ids, expert_count, capacity):
    row_count, top_count = route_ids.shape
    onehot = route_ids[:, :, None] == jnp.arange(expert_count, dtype=jnp.int32)[None, None, :]
    hit_count = jnp.sum(onehot.astype(jnp.int32), 1)
    slot_place = jnp.cumsum(hit_count, 0) - 1
    within = jnp.take_along_axis(slot_place, route_ids, 1)
    dest_slot = route_ids * capacity + within
    pair_count = row_count * top_count
    source = (
        jnp.full((expert_count * capacity,), pair_count, jnp.int32)
        .at[dest_slot.reshape(-1)]
        .set(jnp.arange(pair_count, dtype=jnp.int32))
    )
    live_slot = source < pair_count
    token_row = jnp.minimum(source, pair_count - 1) // top_count
    return (onehot, dest_slot, source, live_slot, token_row)


def per_device(
    tokens,
    teacher,
    valid_mask,
    routes,
    first_gain,
    query_weight,
    key_matrix,
    value_matrix,
    output_weight,
    second_gain,
    router_weight,
    expert_in,
    expert_out,
):
    row_count = tokens.shape[0]
    model_width = tokens.shape[1]
    half_width = model_width // 2
    local_query = query_weight.shape[1] // HEAD_DIM
    local_kv = key_matrix.shape[1] // HEAD_DIM
    query_group_size = local_query // local_kv
    expert_count = router_weight.shape[1]
    row_local = expert_in.shape[0]
    senders = lax.axis_size("expert")
    partner_step = senders // 2
    capacity = 3 * row_count * TOP // (2 * expert_count)
    pair_count = row_count * TOP
    score_rows = min(512, row_count)
    valid_total = lax.psum(jnp.sum(valid_mask).astype(jnp.float32), "expert")
    tokens_f32 = tokens.astype(jnp.float32)
    scale_one = lax.rsqrt(jnp.mean(tokens_f32 * tokens_f32, -1, keepdims=True) + EPS)
    unit_one = tokens_f32 * scale_one
    first_normed = (unit_one * first_gain).astype(jnp.bfloat16)
    cosine_lookup, sine_lookup = rope_tables(row_count, HEAD_DIM)
    query_linear = jnp.dot(first_normed, query_weight, preferred_element_type=jnp.float32).reshape(
        row_count, local_query, HEAD_DIM
    )
    keys_linear = jnp.dot(first_normed, key_matrix, preferred_element_type=jnp.float32).reshape(
        row_count, local_kv, HEAD_DIM
    )
    value_low = jnp.dot(first_normed, value_matrix, preferred_element_type=jnp.float32).astype(
        jnp.bfloat16
    )
    value_low = value_low.reshape(row_count, local_kv, HEAD_DIM)
    query_rotated = apply_rotary(query_linear, cosine_lookup, sine_lookup).astype(jnp.bfloat16)
    keys_rot = apply_rotary(keys_linear, cosine_lookup, sine_lookup).astype(jnp.bfloat16)
    block_of = jnp.arange(row_count, dtype=jnp.int32) // BLOCK

    def scores(start_row):
        stop_row = start_row + score_rows
        query_block = query_rotated.reshape(score_rows, local_kv, query_group_size, HEAD_DIM)
        score_block = (
            jnp.einsum("qhgd,khd->hgqk", query_block, keys_rot, preferred_element_type=jnp.float32)
            * ATTN_SCALE
        )
        allowed = block_of[None, :stop_row] <= block_of[start_row:stop_row, None]
        return (query_block, jnp.where(allowed, score_block, -1e30))

    attn_parts, row_peaks, row_totals = ([], [], [])
    start_row = 0
    query_block, score_block = scores(start_row)
    row_peak = jnp.max(score_block, -1, keepdims=True)
    exp_scores = jnp.exp(score_block - row_peak)
    row_total = jnp.sum(exp_scores, -1, keepdims=True)
    attn_probs = (exp_scores / row_total).astype(jnp.bfloat16)
    attn_parts.append(
        jnp.einsum("hgqk,khd->qhgd", attn_probs, value_low, preferred_element_type=jnp.float32)
    )
    row_peaks.append(row_peak)
    row_totals.append(row_total)
    attended = attn_parts[0].reshape(row_count, local_query * HEAD_DIM).astype(jnp.bfloat16)
    attn_part = jnp.dot(attended, output_weight, preferred_element_type=jnp.float32)
    attn_sum = lax.psum(attn_part, "tensor")
    hidden_state = tokens_f32 + RESIDUAL * attn_sum
    scale_two = lax.rsqrt(jnp.mean(hidden_state * hidden_state, -1, keepdims=True) + EPS)
    unit_two = hidden_state * scale_two
    normed_two = (unit_two * second_gain).astype(jnp.bfloat16)
    router_logits = jnp.dot(normed_two, router_weight, preferred_element_type=jnp.float32)
    onehot, dest_slot, source, live_slot, token_row = slot_tables(routes, expert_count, capacity)
    picked = jnp.sum(jnp.where(onehot, router_logits[:, None, :], 0.0), -1)
    gate_probs = normalize(picked)

    def slot_rows(slot_values):
        split_rows = slot_values.reshape(expert_count, capacity, 2, half_width).transpose(
            2, 0, 1, 3
        )
        return split_rows.reshape(senders, row_local, capacity, half_width)

    def slot_columns(returned, width):
        joined = returned.reshape(2, expert_count, capacity, width).transpose(1, 2, 0, 3)
        return joined.reshape(expert_count * capacity, 2, width)

    send_rows = slot_rows(
        jnp.where(live_slot[:, None], normed_two[token_row], jnp.zeros((), jnp.bfloat16))
    )
    received = lax.all_to_all(send_rows, "expert", split_axis=0, concat_axis=2, tiled=True)
    expert_rows = received.reshape(row_local, senders * capacity, half_width)
    gate_up_part = jnp.einsum(
        "rmd,rcdf->rmcf", expert_rows, expert_in, preferred_element_type=jnp.float32
    )
    gate_up_pre = gate_up_part + shifted(gate_up_part, "expert", partner_step)
    gate_pre = gate_up_pre[:, :, 0]
    up_pre = gate_up_pre[:, :, 1]
    inner_act = (jax.nn.silu(gate_pre) * up_pre).astype(jnp.bfloat16)
    expert_result = jnp.einsum(
        "rmf,rfd->rmd", inner_act, expert_out, preferred_element_type=jnp.float32
    )
    expert_result = expert_result.astype(jnp.bfloat16).reshape(
        row_local, senders, capacity, half_width
    )
    returned = lax.all_to_all(expert_result, "expert", split_axis=1, concat_axis=0, tiled=True)
    per_route = slot_columns(returned, half_width).reshape(expert_count * capacity, model_width)[
        dest_slot
    ]
    moe_part = jnp.sum(gate_probs[:, :, None] * per_route, 1)
    moe_sum = lax.psum(moe_part, "tensor")
    output = hidden_state + RESIDUAL * moe_sum
    residual_err = output - teacher.astype(jnp.float32)
    valid_rows = valid_mask.astype(jnp.float32)
    squared_local = jnp.sum(valid_rows * jnp.sum(residual_err * residual_err, -1))
    token_total = senders * row_count
    grad_out = token_total / valid_total * valid_rows[:, None] * residual_err
    grad_moe = (RESIDUAL * grad_out).astype(jnp.bfloat16)
    gate_part = jnp.einsum("td,tkd->tk", grad_moe, per_route, preferred_element_type=jnp.float32)
    gate_slot = gate_probs.reshape(pair_count)[jnp.minimum(source, pair_count - 1)]
    grad_slots = jnp.where(live_slot[:, None], gate_slot[:, None] * grad_moe[token_row], 0.0)
    grad_received = lax.all_to_all(
        slot_rows(grad_slots.astype(jnp.bfloat16)),
        "expert",
        split_axis=0,
        concat_axis=2,
        tiled=True,
    )
    grad_expert = grad_received.reshape(row_local, senders * capacity, half_width)
    grad_inner_part = jnp.einsum(
        "rmd,rfd->rmf", grad_expert, expert_out, preferred_element_type=jnp.float32
    )
    grad_inner = grad_inner_part + shifted(grad_inner_part, "expert", partner_step)
    grad_expert_out = jnp.einsum(
        "rmf,rmd->rfd", inner_act, grad_expert, preferred_element_type=jnp.float32
    )
    sigmoid_gate = jax.nn.sigmoid(gate_pre)
    grad_gate = grad_inner * up_pre * sigmoid_gate * (1.0 + gate_pre * (1.0 - sigmoid_gate))
    grad_up = grad_inner * (gate_pre * sigmoid_gate)
    grad_pre = jnp.stack([grad_gate, grad_up], 2).astype(jnp.bfloat16)
    grad_expert_in = jnp.einsum(
        "rmd,rmcf->rcdf", expert_rows, grad_pre, preferred_element_type=jnp.float32
    )
    grad_slot_rows = jnp.einsum(
        "rmcf,rcdf->rmd", grad_pre, expert_in, preferred_element_type=jnp.float32
    )
    grad_slot_rows = grad_slot_rows.astype(jnp.bfloat16).reshape(
        row_local, senders, capacity, half_width
    )
    grad_back = lax.all_to_all(grad_slot_rows, "expert", split_axis=1, concat_axis=0, tiled=True)
    grad_back = slot_columns(grad_back, half_width).reshape(expert_count * capacity, model_width)
    grad_two_part = jnp.sum(grad_back[dest_slot].astype(jnp.float32), 1)
    grad_two_experts, grad_gates = lax.psum((grad_two_part, gate_part), "tensor")
    grad_picked = gate_probs * (grad_gates - jnp.sum(gate_probs * grad_gates, -1, keepdims=True))
    grad_logits = jnp.sum(jnp.where(onehot, grad_picked[:, :, None], 0.0), 1).astype(jnp.bfloat16)
    grad_router = jnp.einsum(
        "td,te->de", normed_two, grad_logits, preferred_element_type=jnp.float32
    )
    grad_two = grad_two_experts + jnp.einsum(
        "te,de->td", grad_logits, router_weight, preferred_element_type=jnp.float32
    )
    grad_second_gain = jnp.sum(grad_two * unit_two, 0)
    grad_unit_two = grad_two * second_gain
    grad_hidden = grad_out + scale_two * (
        grad_unit_two - unit_two * jnp.mean(grad_unit_two * unit_two, -1, keepdims=True)
    )
    grad_attn = (RESIDUAL * grad_hidden).astype(jnp.bfloat16)
    grad_output = jnp.einsum("tc,td->cd", attended, grad_attn, preferred_element_type=jnp.float32)
    grad_attended = jnp.einsum(
        "td,cd->tc", grad_attn, output_weight, preferred_element_type=jnp.float32
    )
    grad_attended = grad_attended.astype(jnp.bfloat16).reshape(
        row_count, local_kv, query_group_size, HEAD_DIM
    )
    grad_query_parts = []
    grad_keys = jnp.zeros((row_count, local_kv, HEAD_DIM), jnp.float32)
    grad_values = jnp.zeros((row_count, local_kv, HEAD_DIM), jnp.float32)
    for block_index, start_row in enumerate(range(0, row_count, score_rows)):
        stop_row = start_row + score_rows
        query_block, score_block = scores(start_row)
        attn_probs = jnp.exp(score_block - row_peaks[block_index]) / row_totals[block_index]
        probs_low = attn_probs.astype(jnp.bfloat16)
        grad_probs = jnp.einsum(
            "qhgd,khd->hgqk", grad_attended, value_low, preferred_element_type=jnp.float32
        )
        grad_scores = attn_probs * (
            grad_probs - jnp.sum(attn_probs * grad_probs, -1, keepdims=True)
        )
        grad_scores = grad_scores.astype(jnp.bfloat16)
        grad_query_parts.append(
            ATTN_SCALE
            * jnp.einsum(
                "hgqk,khd->qhgd", grad_scores, keys_rot, preferred_element_type=jnp.float32
            )
        )
        grad_keys = grad_keys.at[:stop_row].add(
            ATTN_SCALE
            * jnp.einsum(
                "hgqk,qhgd->khd", grad_scores, query_block, preferred_element_type=jnp.float32
            )
        )
        grad_values = grad_values.at[:stop_row].add(
            jnp.einsum(
                "hgqk,qhgd->khd", probs_low, grad_attended, preferred_element_type=jnp.float32
            )
        )
    grad_query_rot = grad_query_parts[0].reshape(row_count, local_query, HEAD_DIM)
    grad_query_low = unrotate(grad_query_rot, cosine_lookup, sine_lookup).reshape(
        row_count, local_query * HEAD_DIM
    )
    grad_query_low = grad_query_low.astype(jnp.bfloat16)
    grad_keys_low = unrotate(grad_keys, cosine_lookup, sine_lookup).reshape(
        row_count, local_kv * HEAD_DIM
    )
    grad_keys_low = grad_keys_low.astype(jnp.bfloat16)
    grad_values_low = grad_values.reshape(row_count, local_kv * HEAD_DIM).astype(jnp.bfloat16)
    grad_query = jnp.einsum(
        "td,tc->dc", first_normed, grad_query_low, preferred_element_type=jnp.float32
    )
    grad_key = jnp.einsum(
        "td,tc->dc", first_normed, grad_keys_low, preferred_element_type=jnp.float32
    )
    grad_value = jnp.einsum(
        "td,tc->dc", first_normed, grad_values_low, preferred_element_type=jnp.float32
    )
    grad_one_part = (
        jnp.einsum("tc,dc->td", grad_query_low, query_weight, preferred_element_type=jnp.float32)
        + jnp.einsum("tc,dc->td", grad_keys_low, key_matrix, preferred_element_type=jnp.float32)
        + jnp.einsum("tc,dc->td", grad_values_low, value_matrix, preferred_element_type=jnp.float32)
    )
    grad_one = lax.psum(grad_one_part.astype(jnp.bfloat16), "tensor").astype(jnp.float32)
    grad_first_gain = jnp.sum(grad_one * unit_one, 0)
    grad_unit_one = grad_one * first_gain
    grad_tokens = grad_hidden + scale_one * (
        grad_unit_one - unit_one * jnp.mean(grad_unit_one * unit_one, -1, keepdims=True)
    )
    reduced = lax.psum(
        (
            grad_first_gain,
            grad_query,
            grad_key,
            grad_value,
            grad_output,
            grad_second_gain,
            grad_router,
            squared_local,
        ),
        "expert",
    )
    loss_value = reduced[7] / (2.0 * model_width * valid_total)
    return (
        output.astype(jnp.bfloat16),
        loss_value,
        grad_tokens,
        reduced[0],
        reduced[1],
        reduced[2],
        reduced[3],
        reduced[4],
        reduced[5],
        reduced[6],
        grad_expert_in,
        grad_expert_out,
    )


def solution(mesh):
    return jax.shard_map(
        per_device,
        mesh=mesh,
        in_specs=(
            P("expert", None),
            P("expert", None),
            P("expert"),
            P("expert", None),
            P(),
            P(None, "tensor"),
            P(None, "tensor"),
            P(None, "tensor"),
            P("tensor", None),
            P(),
            P(),
            P("expert", None, None, "tensor"),
            P("expert", "tensor", None),
        ),
        out_specs=(
            P("expert", None),
            P(),
            P("expert", None),
            P(),
            P(None, "tensor"),
            P(None, "tensor"),
            P(None, "tensor"),
            P("tensor", None),
            P(),
            P(),
            P("expert", None, None, "tensor"),
            P("expert", "tensor", None),
        ),
        check_vma=False,
    )
```

profile of v0, /device:TPU:0, one launch (start us, length us, event | category | flops | bytes accessed | tf_op | source)
XLA Modules:
  0.0 2694.3 jit_solution(5498400139283303845)
XLA Ops:
  7.3 1.7 fusion.27
  10.2 2.5 convolution_convert_fusion.3
  14.2 4.7 fusion.80
  18.9 2.8 convolution_convert_fusion.2
  22.4 1.8 fusion.81
  26.2 33.0 %gather_fusion.5 = s32[4096]{0:T(1024)S(1)} fusion(s32[512,32]{0,1:T(8,128)S(1)} %bitcast_bitcast_fusion, s32[4096]{0:T(1024)S(1)} %reshape.422), kind=kCustom, calls=%fused_computation.5 | custom fusion | bytes 65536 | tf_op jit(solution)/shard_map/jit(take_along_axis)/gather | solution.py:63
  60.4 15.5 scatter_custom_fusion
  76.1 2.4 all-reduce.8.cloned.1.call-done
  78.5 2.0 multiply_reduce_fusion.4
  82.1 26.9 gather_fusion
  109.0 21.2 gather.23
  130.3 7.5 copy_select_fusion
  137.8 278.8 %all_to_all.60 = bf16[8,8,192,512]{3,2,1,0:T(8,128)(2,1)S(1)} all-to-all(bf16[8,8,192,512]{3,2,1,0:T(8,128)(2,1)S(1)} %bitcast.210), channel_id=1, replica_groups=mesh['expert'=8,'tensor'=4] {'expert'}, dimensions={0} | all-to-all | bytes 25165824 | tf_op jit(solution)/shard_map/all_to_all | solution.py:171
  416.6 5.2 copy.100
  421.8 12.5 fusion.83
  434.9 540.7 %collective-permute-done = f32[8,1536,2,128]{3,1,2,0:T(8,128)S(1)} collective-permute-done((f32[8,1536,2,128]{3,1,2,0:T(8,128)}, f32[8,1536,2,128]{3,1,2,0:T(8,128)S(1)}, u32[]{:S(2)}, u32[]{:S(2)}) %collective-permute-start) | collective-permute-done | bytes 12582944 | tf_op jit(solution)/shard_map/ppermute | solution.py:18
  975.6 5.7 add.164
  981.3 4.5 copy-done.5
  985.8 1.7 multiply_convert_fusion.2
  987.5 6.3 convolution_convert_fusion
  993.7 10.7 copy.102
  1004.4 5.5 all-to-all-start.1
  1013.6 269.8 %all-to-all-done.1 = bf16[8,8,192,512]{3,2,0,1:T(8,128)(2,1)} async-done(((bf16[8,8,192,512]{3,2,0,1:T(8,128)(2,1)}), bf16[8,8,192,512]{3,2,0,1:T(8,128)(2,1)}, u32[]{:S(2)}, u32[]{:S(2)}) %all-to-all-start.1) | async-done | bytes 12582944 | tf_op jit(solution)/shard_map/all_to_all | solution.py:186
  1283.3 23.0 copy.103
  1306.4 7.0 copy.134
  1313.4 27.1 %gather_fusion.1 = bf16[4096,1024]{1,0:T(8,128)(2,1)} fusion(bf16[6144,1024]{1,0:T(8,128)(2,1)} %bitcast.205, s32[4096]{0:T(1024)S(1)} %broadcast_clamp_fusion), kind=kCustom, calls=%fused_computation.1 | custom fusion | bytes 16793600 | tf_op jit(solution)/shard_map/gather | solution.py:187
  1340.5 9.8 multiply_reduce_fusion
  1351.7 20.1 psum.101
  1372.7 34.3 %gather_fusion.2 = f32[6144]{0:T(1024)S(1)} fusion(f32[4096]{0:T(1024)S(1)} %div.124, s32[6144]{0:T(1024)S(1)} %get-tuple-element.129), kind=kCustom, calls=%fused_computation.2 | custom fusion | bytes 73728 | tf_op jit(solution)/shard_map/gather | solution.py:200
  1407.1 3.0 multiply_convert_fusion.4
  1410.1 26.9 gather_fusion.3
  1437.0 31.3 %reshape.381 = f32[32,192,2,512]{3,2,1,0:T(2,128)} reshape(bf16[6144,1024]{1,0:T(8,128)(2,1)} %gather_fusion.3) | data formatting | bytes 37748736 | tf_op jit(solution)/shard_map/convert_element_type | solution.py:201
  1468.2 13.5 fusion.2
  1481.8 272.4 %all_to_all.61 = bf16[8,8,192,512]{3,2,1,0:T(8,128)(2,1)S(1)} all-to-all(bf16[8,8,192,512]{3,2,1,0:T(8,128)(2,1)S(1)} %bitcast.217), channel_id=1, replica_groups=mesh['expert'=8,'tensor'=4] {'expert'}, dimensions={0} | all-to-all | bytes 25165824 | tf_op jit(solution)/shard_map/all_to_all | solution.py:202
  1754.1 1.8 copy.107
  1756.0 5.9 fusion.84
  1762.4 1.7 collective-permute-start.1
  1764.1 269.5 %collective-permute-done.1 = f32[8,1536,128]{2,1,0:T(8,128)} collective-permute-done((f32[8,1536,128]{2,1,0:T(8,128)}, f32[8,1536,128]{2,1,0:T(8,128)}, u32[]{:S(2)}, u32[]{:S(2)}) %collective-permute-start.1) | collective-permute-done | bytes 6291488 | tf_op jit(solution)/shard_map/ppermute | solution.py:18
  2033.6 12.6 fusion.17
  2046.2 10.8 bitcast_convert_fusion
  2057.0 6.6 copy.109
  2063.6 276.9 %all_to_all.62 = bf16[8,8,192,512]{3,2,0,1:T(8,128)(2,1)S(1)} all-to-all(bf16[8,8,192,512]{3,2,0,1:T(8,128)(2,1)S(1)} %copy.109), channel_id=1, replica_groups=mesh['expert'=8,'tensor'=4] {'expert'}, dimensions={1} | all-to-all | bytes 25165824 | tf_op jit(solution)/shard_map/all_to_all | solution.py:230
  2340.5 49.8 %copy.110 = bf16[32,192,2,512]{3,2,1,0:T(2,128)(2,1)S(1)} copy(bf16[32,192,2,512]{3,1,0,2:T(8,128)(2,1)S(1)} %bitcast.214) | data formatting | bytes 25165824 | tf_op jit(solution)/shard_map/transpose | solution.py:165
  2390.3 7.0 copy.135
  2397.3 27.1 %gather_fusion.4 = bf16[4096,1024]{1,0:T(8,128)(2,1)} fusion(bf16[6144,1024]{1,0:T(8,128)(2,1)} %bitcast.204, s32[4096]{0:T(1024)S(1)} %broadcast_clamp_fusion), kind=kCustom, calls=%fused_computation.4 | custom fusion | bytes 16793600 | tf_op jit(solution)/shard_map/gather | solution.py:232
  2424.4 11.9 convert_reduce_fusion
  2436.8 8.7 fusion.3
  2445.6 11.6 psum.103
  2458.3 28.1 %all-reduce.12.cloned.1.call-done = f32[512,1024]{1,0:T(8,128)} async-done(((f32[512,1024]{1,0:T(8,128)}), f32[512,1024]{1,0:T(8,128)}) %all-reduce.12.cloned.1.call-update) | async-done | bytes 2097168 | tf_op jit(solution)/shard_map/psum | solution.py:233
  2486.5 5.0 multiply_reduce_fusion.1
  2491.6 1.9 multiply_add_fusion
  2500.9 1.6 fusion.73
  2503.0 1.5 add_convert_fusion
  2506.4 1.4 fusion.41
  2508.5 9.2 fusion.87
  2517.7 10.1 fusion.19
  2527.8 5.5 copy.116
  2533.9 7.2 all-reduce.14.cloned.1.call-done
  2541.1 2.0 fusion.26
  2543.1 23.5 all-reduce
  2567.3 3.8 fusion.23
  2571.1 108.7 %all-reduce.16.cloned.1.call-done = (f32[1024,256]{1,0:T(8,128)}, f32[1024,128]{1,0:T(8,128)}, f32[1024,128]{1,0:T(8,128)}, f32[256,1024]{1,0:T(8,128)}, f32[1024,32]{0,1:T(8,128)}) async-done(((f32[1024,256]{1,0:T(8,128)}, f32[1024,128]{1,0:T(8,128)}, f32[1024,128]{1,0:T(8,128)}, f32[256,1024]{1,0:T(8,128)}, f32[1024,32]{0,1:T(8,128)}), (f32[1024,256]{1,0:T(8,128)}, f32[1024,128]{1,0:T(8,128)}, ...) | async-done | bytes 3276816 | tf_op jit(solution)/shard_map/psum | solution.py:317
  2679.8 2.4 copy.161
  2682.2 1.9 copy.162
  (222 shorter events, 28.0 us)
Async XLA Ops:
  7.2 414.7 %copy-start = (bf16[8,2,512,128]{3,2,1,0:T(8,128)(2,1)S(1)}, bf16[8,2,512,128]{3,2,1,0:T(8,128)(2,1)}, u32[]{:S(2)}) copy-start(bf16[8,2,512,128]{3,2,1,0:T(8,128)(2,1)} %param.32) | copy-start | bytes 6291460
  7.2 5.6 copy-start.12
  7.2 5.6 copy-start.64
  7.2 5.5 copy-start.43
  7.2 71.3 %all-reduce.8.cloned.1.call-start = ((), (), s32[]{:S(2)}) async-start(), calls=%async_computation.4 | async-start | bytes 4194304 | tf_op jit(solution)/shard_map/psum | solution.py:148
  7.3 6.1 copy-start.31
  9.0 5.0 copy-start.62
  9.3 4.7 copy-start.22
  9.3 4.7 copy-start.24
  14.0 4.8 copy-start.45
  14.0 4.8 copy-start.47
  14.2 4.7 copy-start.33
  14.2 4.7 copy-start.35
  18.9 2.8 copy-start.67
  18.9 3.5 copy-start.20
  21.8 2.5 copy-start.38
  59.4 22.5 copy-start.52
  80.5 28.5 %copy-start.56 = (f32[512]{0:T(512)}, f32[512]{0:T(512)S(1)}, u32[]{:S(2)}) copy-start(f32[512]{0:T(512)S(1)} %add_rsqrt_fusion) | copy-start | bytes 6148
  82.1 930.8 %copy-start.1 = (bf16[512,1024]{1,0:T(8,128)(2,1)}, bf16[512,1024]{1,0:T(8,128)(2,1)S(1)}, u32[]{:S(2)}) copy-start(bf16[512,1024]{1,0:T(8,128)(2,1)S(1)} %multiply_convert_fusion.5) | copy-start | bytes 3145732
  434.4 541.2 %collective-permute-start = (f32[8,1536,2,128]{3,1,2,0:T(8,128)}, f32[8,1536,2,128]{3,1,2,0:T(8,128)S(1)}, u32[]{:S(2)}, u32[]{:S(2)}) collective-permute-start(f32[8,1536,2,128]{3,1,2,0:T(8,128)} %fusion.83), channel_id=1, source_target_pairs={{0,16},{4,20},{8,24},{12,28},{16,0},{20,4},{24,8},{28,12},{1,17},{... | collective-permute-start | bytes 37748744 | tf_op jit(solution)/shard_map/ppermute | solution.py:18
  981.3 4.5 copy-start.5
  987.4 6.3 copy-start.10
  1004.4 8.4 copy-start.40
  1004.4 278.9 %all-to-all-start.1 = ((bf16[8,8,192,512]{3,2,0,1:T(8,128)(2,1)}), bf16[8,8,192,512]{3,2,0,1:T(8,128)(2,1)}, u32[]{:S(2)}, u32[]{:S(2)}) async-start(bf16[8,8,192,512]{3,2,0,1:T(8,128)(2,1)} %copy.102), calls=%async_computation.1 | async-start | bytes 25165824 | tf_op jit(solution)/shard_map/all_to_all | solution.py:186
  1009.9 397.1 %all-reduce.10.cloned.1.call-start = ((), (), s32[]{:S(2)}) async-start(), calls=%async_computation.5 | async-start | bytes 4194304 | tf_op jit(solution)/shard_map/psum | solution.py:191
  1013.4 293.0 %copy-start.29 = (f32[512,8]{0,1:T(8,128)}, f32[512,8]{0,1:T(8,128)S(1)}, u32[]{:S(2)}) copy-start(f32[512,8]{0,1:T(8,128)S(1)} %select_reduce_fusion.1) | copy-start | bytes 49156
  1013.4 293.0 %copy-start.50 = (f32[512]{0:T(512)}, f32[512]{0:T(512)S(1)}, u32[]{:S(2)}) copy-start(f32[512]{0:T(512)S(1)} %reduce_max.19) | copy-start | bytes 6148
  1013.4 292.9 %copy-start.54 = (f32[512]{0:T(512)}, f32[512]{0:T(512)S(1)}, u32[]{:S(2)}) copy-start(f32[512]{0:T(512)S(1)} %fusion.53) | copy-start | bytes 6148
  1340.5 9.9 copy-start.60
  1350.3 1136.1 %all-reduce.12.cloned.1.call-start = ((), (), s32[]{:S(2)}) async-start(), calls=%async_computation.6 | async-start | bytes 4194304 | tf_op jit(solution)/shard_map/psum | solution.py:233
  1372.5 34.5 %copy-start.58 = (f32[512]{0:T(512)}, f32[512]{0:T(512)S(1)}, u32[]{:S(2)}) copy-start(f32[512]{0:T(512)S(1)} %convert_multiply_fusion.3) | copy-start | bytes 6148
  1410.1 26.9 copy-start.3
  1756.0 6.4 copy-start.4
  1762.4 271.2 %collective-permute-start.1 = (f32[8,1536,128]{2,1,0:T(8,128)}, f32[8,1536,128]{2,1,0:T(8,128)}, u32[]{:S(2)}, u32[]{:S(2)}) collective-permute-start(f32[8,1536,128]{2,1,0:T(8,128)} %fusion.84), channel_id=1, source_target_pairs={{0,16},{4,20},{8,24},{12,28},{16,0},{20,4},{24,8},{28,12},{1,17},{... | collective-permute-start | bytes 18874376 | tf_op jit(solution)/shard_map/ppermute | solution.py:18
  2436.3 104.8 %all-reduce.14.cloned.1.call-start = ((), (), s32[]{:S(2)}) async-start(), calls=%async_computation.7 | async-start | bytes 2097152 | tf_op jit(solution)/shard_map/psum | solution.py:311
  2436.7 20.5 copy-start.30
  2436.7 20.5 copy-start.51
  2436.8 20.5 copy-start.55
  2436.8 20.5 copy-start.39
  2436.8 20.6 copy-start.2
  2436.8 49.7 %copy-start.41 = (bf16[1024,32]{0,1:T(8,128)(2,1)S(1)}, bf16[1024,32]{0,1:T(8,128)(2,1)}, u32[]{:S(2)}) copy-start(bf16[1024,32]{0,1:T(8,128)(2,1)} %param.31) | copy-start | bytes 196612
  2436.8 49.7 %copy-start.53 = (f32[1024]{0:T(1024)S(1)}, f32[1024]{0:T(1024)}, u32[]{:S(2)}) copy-start(f32[1024]{0:T(1024)} %param.30) | copy-start | bytes 12292
  2436.8 49.6 %copy-start.57 = (f32[512]{0:T(512)S(1)}, f32[512]{0:T(512)}, u32[]{:S(2)}) copy-start(f32[512]{0:T(512)} %copy-done.56) | copy-start | bytes 6148
  2458.3 33.2 %copy-start.14 = (bf16[512,1024]{1,0:T(8,128)(2,1)S(1)}, bf16[512,1024]{1,0:T(8,128)(2,1)}, u32[]{:S(2)}) copy-start(bf16[512,1024]{1,0:T(8,128)(2,1)} %param.22) | copy-start | bytes 3145732
  2458.3 33.2 %copy-start.59 = (f32[512]{0:T(512)S(1)}, f32[512]{0:T(512)}, u32[]{:S(2)}) copy-start(f32[512]{0:T(512)} %copy-done.58) | copy-start | bytes 6148
  2486.5 5.0 copy-start.7
  2486.5 5.0 copy-start.11
  2491.5 2.7 copy-start.17
  2491.5 2.7 copy-start.68
  2494.3 2.6 copy-start.42
  2495.1 2.3 copy-start.70
  2498.2 2.0 copy-start.46
  2500.2 2.3 copy-start.44
  2500.8 2.1 copy-start.32
  2503.0 3.2 copy-start.28
  2504.5 175.2 %all-reduce.16.cloned.1.call-start = ((), (), s32[]{:S(2)}) async-start(), calls=%async_computation.8 | async-start | bytes 6553600 | tf_op jit(solution)/shard_map/psum | solution.py:317
  2508.5 9.2 copy-start.18
  2508.5 9.2 copy-start.19
  2527.8 5.5 copy-start.61
  2527.8 5.5 copy-start.69
  2527.8 15.3 copy-start.66
  2679.8 4.3 copy-start.37
  2679.8 5.1 copy-start.26
  2679.8 6.0 copy-start.49
  (15 other events, 21.4 us)
Sparse Core Ops, SparseCore 0:
  24.4 54.1 all-reduce.7
  1350.5 49.7 all-reduce.9
  2436.4 50.0 all-reduce.11
  2504.7 36.3 all-reduce.13
  2545.7 134.0 all-reduce.15
where the time goes:
time: 2700 us; the launch traced here: 2690 us
  waiting for transfers between devices  1230 us (46%)
  blocking collectives  883 us (33%)
  local copies, waits for them, and re-layouts  378 us (14%)
  matrix products  94.3 us (3%)
  other arithmetic  84.3 us (3%)
    ppermute x2, waiting for transfers between devices, shifted(): return lax.ppermute(value, axis, pairs)  810 us
    all_to_all x1, blocking collectives, per_device(): lax.all_to_all(send_rows, 'expert', split_axis=0, concat_axis=2, tiled=True)  279 us
    all_to_all x1, blocking collectives, per_device(): lax.all_to_all(grad_slot_rows, 'expert', split_axis=1, concat_axis=0, til...  277 us
    all_to_all x1, blocking collectives, per_device(): lax.all_to_all(slot_rows(grad_slots.astype(jnp.bfloat16)), 'expert', spli...  272 us
    all_to_all x1, waiting for transfers between devices, per_device(): lax.all_to_all(expert_result, 'expert', split_axis=1, concat_axis=0, tile...  270 us
    psum x1, waiting for transfers between devices, per_device(): lax.psum((grad_first_gain, grad_query, grad_key, grad_value, grad_output,...  109 us
    transpose x2, local copies, waits for them, and re-layouts, slot_columns(): returned.reshape(2, expert_count, capacity, width).transpose(1, 2, 0, 3)  72.8 us
  transfers between devices with their start and end apart: 8, of which 7 were waited for; matrix products, arithmetic and copies ran while one was open for 5% of the time, Pallas kernels for 0%

commit v1 on v0

--- a/solution.py
+++ b/solution.py
@@ -10,6 +10,39 @@
 ATTN_SCALE = 0.015625
 RESIDUAL = 0.22
 THETA = 10000.0
+
+
+def direct_bench_for(xs, join_dim, my_tile):
+    after = xs.shape
+    back = xs.reshape(
+        *after[:join_dim], my_tile, after[join_dim] // my_tile, *after[join_dim + 1 :]
+    )
+    field_out = jnp.moveaxis(back, join_dim, 0)
+    return field_out
+
+
+def bind_spot_up(work_x, dim_no):
+    work_x = jnp.moveaxis(work_x, 0, dim_no)
+    low = work_x.shape
+    before = work_x.reshape(*low[:dim_no], low[dim_no] * low[dim_no + 1], *low[dim_no + 2 :])
+    return before
+
+
+def direct_slices(inp, own_rows, u, device_axis):
+    near, f_now = (lax.psum(1, axis_name=device_axis), lax.axis_index(device_axis))
+    t_next = direct_bench_for(u, own_rows, near)
+    k_now = t_next
+    for j0 in range(1, near):
+        z, spare = ((f_now + j0) % near, (f_now - j0) % near)
+        x_next = lax.dynamic_index_in_dim(t_next, z, 0)
+        e_now = lax.ppermute(
+            x_next,
+            axis_name=device_axis,
+            perm=list(map(lambda j: (j, (j + j0) % near), range(near))),
+        )
+        k_now = lax.dynamic_update_slice_in_dim(k_now, e_now, spare, axis=0)
+    response = bind_spot_up(k_now, inp)
+    return response
 
 
 def shifted(value, axis, steps):
@@ -183,7 +216,7 @@
     expert_result = expert_result.astype(jnp.bfloat16).reshape(
         row_local, senders, capacity, half_width
     )
-    returned = lax.all_to_all(expert_result, "expert", split_axis=1, concat_axis=0, tiled=True)
+    returned = direct_slices(0, 1, expert_result, "expert")
     per_route = slot_columns(returned, half_width).reshape(expert_count * capacity, model_width)[
         dest_slot
     ]

time: 2700 us -> 2730 us (1.011)
  waiting for transfers between devices: 1230 us -> 1130 us
  blocking collectives: 883 us -> 956 us
  local copies, waits for them, and re-layouts: 378 us -> 419 us
    all_to_all x1 -> x0, waiting for transfers between devices: 270 us -> none  [per_device(): lax.all_to_all(expert_result, 'expert', split_axis=1, concat_axis=0, tile...]
    ppermute x0 -> x7, waiting for transfers between devices: none -> 177 us  [direct_slices(): lax.ppermute(x_next, axis_name=device_axis, perm=list(map(lambda j: (j, (...]
    psum x1, blocking collectives: 20.1 us -> 93 us  [per_device(): valid_total = lax.psum(jnp.sum(valid_mask).astype(jnp.float32), 'expert')]
  transfers between devices with their start and end apart: 8 -> 14, of which waited for: 7 -> 10; matrix products, arithmetic and copies ran while one was open for 5% -> 5% of each run, Pallas kernels for 0% -> 0%
where the time goes in v1:
time: 2730 us; the launch traced here: 2720 us
  waiting for transfers between devices  1130 us (41%)
  blocking collectives  956 us (35%)
  local copies, waits for them, and re-layouts  419 us (15%)
  matrix products  94.2 us (3%)
  other arithmetic  87.5 us (3%)
    ppermute x2, waiting for transfers between devices, shifted(): return lax.ppermute(value, axis, pairs)  810 us
    all_to_all x1, blocking collectives, per_device(): lax.all_to_all(send_rows, 'expert', split_axis=0, concat_axis=2, tiled=True)  279 us
    all_to_all x1, blocking collectives, per_device(): lax.all_to_all(grad_slot_rows, 'expert', split_axis=1, concat_axis=0, til...  277 us
    all_to_all x1, blocking collectives, per_device(): lax.all_to_all(slot_rows(grad_slots.astype(jnp.bfloat16)), 'expert', spli...  271 us
    ppermute x7, waiting for transfers between devices, direct_slices(): lax.ppermute(x_next, axis_name=device_axis, perm=list(map(lambda j: (j, (...  177 us
    psum x1, waiting for transfers between devices, per_device(): lax.psum((grad_first_gain, grad_query, grad_key, grad_value, grad_output,...  109 us
    transpose x2, local copies, waits for them, and re-layouts, slot_columns(): returned.reshape(2, expert_count, capacity, width).transpose(1, 2, 0, 3)  99.7 us
    psum x1, blocking collectives, per_device(): valid_total = lax.psum(jnp.sum(valid_mask).astype(jnp.float32), 'expert')  93 us
  transfers between devices with their start and end apart: 14, of which 10 were waited for; matrix products, arithmetic and copies ran while one was open for 5% of the time, Pallas kernels for 0%

profile of v1, /device:TPU:0, one launch (start us, length us, event | category | flops | bytes accessed | tf_op | source)
XLA Modules:
  0.0 2719.6 jit_solution(10769241638370363145)
XLA Ops:
  7.3 1.7 fusion.27
  10.2 2.6 convolution_convert_fusion.3
  14.2 4.7 fusion.80
  19.0 2.8 convolution_convert_fusion.2
  22.5 1.8 fusion.81
  26.3 33.0 %gather_fusion.5 = s32[4096]{0:T(1024)S(1)} fusion(s32[512,32]{0,1:T(8,128)S(1)} %bitcast_bitcast_fusion, s32[4096]{0:T(1024)S(1)} %reshape.420), kind=kCustom, calls=%fused_computation.5 | custom fusion | bytes 65536 | tf_op jit(solution)/shard_map/jit(take_along_axis)/gather | solution.py:96
  60.5 15.5 scatter_custom_fusion
  76.3 2.3 all-reduce.8.cloned.1.call-done
  78.6 2.0 multiply_reduce_fusion.4
  82.1 26.7 gather_fusion
  108.9 21.3 gather.23
  130.2 7.5 copy_select_fusion
  137.7 279.0 %all_to_all.45 = bf16[8,8,192,512]{3,2,1,0:T(8,128)(2,1)S(1)} all-to-all(bf16[8,8,192,512]{3,2,1,0:T(8,128)(2,1)S(1)} %bitcast.227), channel_id=1, replica_groups=mesh['expert'=8,'tensor'=4] {'expert'}, dimensions={0} | all-to-all | bytes 25165824 | tf_op jit(solution)/shard_map/all_to_all | solution.py:204
  416.7 5.2 copy.100
  421.9 12.5 fusion.83
  435.0 540.8 %collective-permute-done = f32[8,1536,2,128]{3,1,2,0:T(8,128)} collective-permute-done((f32[8,1536,2,128]{3,1,2,0:T(8,128)}, f32[8,1536,2,128]{3,1,2,0:T(8,128)}, u32[]{:S(2)}, u32[]{:S(2)}) %collective-permute-start) | collective-permute-done | bytes 12582944 | tf_op jit(solution)/shard_map/ppermute | solution.py:51
  975.8 8.9 add.278
  984.7 4.5 copy-done.5
  989.2 1.7 multiply_convert_fusion.2
  990.9 6.3 convolution_convert_fusion
  997.2 8.4 dynamic-slice_bitcast_fusion
  1006.6 2.9 collective-permute-start.3
  1014.1 31.0 %collective-permute-done.2 = bf16[1,8,1,192,512]{4,3,1,0,2:T(8,128)(2,1)} collective-permute-done((bf16[1,8,1,192,512]{4,3,1,0,2:T(8,128)(2,1)}, bf16[1,8,1,192,512]{4,3,1,0,2:T(8,128)(2,1)}, u32[]{:S(2)}, u32[]{:S(2)}) %collective-permute-start.2) | collective-permute-done | bytes 1572896 | tf_op jit(solution)/shard_map/ppermute | solution.py:38
  1045.9 33.4 %collective-permute-done.1 = bf16[1,8,1,192,512]{4,3,1,0,2:T(8,128)(2,1)} collective-permute-done((bf16[1,8,1,192,512]{4,3,1,0,2:T(8,128)(2,1)}, bf16[1,8,1,192,512]{4,3,1,0,2:T(8,128)(2,1)}, u32[]{:S(2)}, u32[]{:S(2)}) %collective-permute-start.1) | collective-permute-done | bytes 1572896 | tf_op jit(solution)/shard_map/ppermute | solution.py:38
  1080.4 6.3 copy.153
  1089.9 89.6 %collective-permute-done.3 = bf16[1,8,1,192,512]{4,3,1,0,2:T(8,128)(2,1)} collective-permute-done((bf16[1,8,1,192,512]{4,3,1,0,2:T(8,128)(2,1)}, bf16[1,8,1,192,512]{4,3,1,0,2:T(8,128)(2,1)}, u32[]{:S(2)}, u32[]{:S(2)}) %collective-permute-start.3) | collective-permute-done | bytes 1572896 | tf_op jit(solution)/shard_map/ppermute | solution.py:38
  1185.8 22.9 collective-permute-done.7
  1210.3 49.9 %copy.103 = bf16[32,192,2,512]{3,2,1,0:T(2,128)(2,1)S(1)} copy(bf16[32,192,2,512]{3,1,0,2:T(8,128)(2,1)S(1)} %bitcast.226) | data formatting | bytes 25165824 | tf_op jit(solution)/shard_map/transpose | solution.py:198
  1260.2 7.0 copy.134
  1267.2 27.0 gather_fusion.1
  1294.2 9.8 multiply_reduce_fusion
  1306.0 93.0 %psum.101 = f32[]{:T(128)} all-reduce(f32[]{:T(128)S(6)} %convert_element_type.123), channel_id=1, replica_groups=mesh['expert'=8,'tensor'=4] {'expert'}, use_global_device_ids=true, to_apply=%region_18.19 | all-reduce | flops 1 | bytes 8 | tf_op jit(solution)/shard_map/psum | solution.py:137
  1399.9 34.3 %gather_fusion.2 = f32[6144]{0:T(1024)S(1)} fusion(f32[4096]{0:T(1024)S(1)} %div.124, s32[6144]{0:T(1024)S(1)} %get-tuple-element.136), kind=kCustom, calls=%fused_computation.2 | custom fusion | bytes 73728 | tf_op jit(solution)/shard_map/gather | solution.py:233
  1434.3 3.0 multiply_convert_fusion.4
  1437.3 26.8 gather_fusion.3
  1464.1 31.3 %reshape.379 = f32[32,192,2,512]{3,2,1,0:T(2,128)} reshape(bf16[6144,1024]{1,0:T(8,128)(2,1)} %gather_fusion.3) | data formatting | bytes 37748736 | tf_op jit(solution)/shard_map/convert_element_type | solution.py:234
  1495.4 13.5 fusion.2
  1508.9 271.5 %all_to_all.46 = bf16[8,8,192,512]{3,2,1,0:T(8,128)(2,1)S(1)} all-to-all(bf16[8,8,192,512]{3,2,1,0:T(8,128)(2,1)S(1)} %bitcast.233), channel_id=1, replica_groups=mesh['expert'=8,'tensor'=4] {'expert'}, dimensions={0} | all-to-all | bytes 25165824 | tf_op jit(solution)/shard_map/all_to_all | solution.py:235
  1780.4 1.8 copy.107
  1782.3 5.9 fusion.84
  1789.8 269.6 %collective-permute-done.8 = f32[8,1536,128]{2,1,0:T(8,128)} collective-permute-done((f32[8,1536,128]{2,1,0:T(8,128)}, f32[8,1536,128]{2,1,0:T(8,128)}, u32[]{:S(2)}, u32[]{:S(2)}) %collective-permute-start.8) | collective-permute-done | bytes 6291488 | tf_op jit(solution)/shard_map/ppermute | solution.py:51
  2059.4 12.6 fusion.17
  2072.0 10.8 bitcast_convert_fusion
  2082.8 6.6 copy.109
  2089.4 276.9 %all_to_all.47 = bf16[8,8,192,512]{3,2,0,1:T(8,128)(2,1)S(1)} all-to-all(bf16[8,8,192,512]{3,2,0,1:T(8,128)(2,1)S(1)} %copy.109), channel_id=1, replica_groups=mesh['expert'=8,'tensor'=4] {'expert'}, dimensions={1} | all-to-all | bytes 25165824 | tf_op jit(solution)/shard_map/all_to_all | solution.py:263
  2366.3 49.8 %copy.110 = bf16[32,192,2,512]{3,2,1,0:T(2,128)(2,1)S(1)} copy(bf16[32,192,2,512]{3,1,0,2:T(8,128)(2,1)S(1)} %bitcast.231) | data formatting | bytes 25165824 | tf_op jit(solution)/shard_map/transpose | solution.py:198
  2416.1 7.1 copy.135
  2423.1 27.0 gather_fusion.4
  2450.1 11.9 convert_reduce_fusion
  2462.3 8.3 fusion.3
  2470.8 11.8 psum.103
  2483.7 29.0 %all-reduce.12.cloned.1.call-done = f32[512,1024]{1,0:T(8,128)} async-done(((f32[512,1024]{1,0:T(8,128)}), f32[512,1024]{1,0:T(8,128)}) %all-reduce.12.cloned.1.call-update) | async-done | bytes 2097168 | tf_op jit(solution)/shard_map/psum | solution.py:266
  2512.7 5.0 multiply_reduce_fusion.1
  2517.7 1.9 multiply_add_fusion
  2527.2 1.6 fusion.73
  2534.8 9.2 fusion.87
  2544.0 10.1 fusion.19
  2554.1 5.4 copy.116
  2560.2 7.2 all-reduce.14.cloned.1.call-done
  2567.3 2.0 fusion.26
  2569.4 23.5 all-reduce
  2593.5 3.8 fusion.23
  2597.3 108.7 %all-reduce.16.cloned.1.call-done = (f32[1024,256]{1,0:T(8,128)}, f32[1024,128]{1,0:T(8,128)}, f32[1024,128]{1,0:T(8,128)}, f32[256,1024]{1,0:T(8,128)}, f32[1024,32]{0,1:T(8,128)}) async-done(((f32[1024,256]{1,0:T(8,128)}, f32[1024,128]{1,0:T(8,128)}, f32[1024,128]{1,0:T(8,128)}, f32[256,1024]{1,0:T(8,128)}, f32[1024,32]{0,1:T(8,128)}), (f32[1024,256]{1,0:T(8,128)}, f32[1024,128]{1,0:T(8,128)}, ...) | async-done | bytes 3276816 | tf_op jit(solution)/shard_map/psum | solution.py:350
  2706.0 2.4 copy.170
  (248 shorter events, 48.1 us)
Async XLA Ops:
  7.2 414.7 %copy-start = (bf16[8,2,512,128]{3,2,1,0:T(8,128)(2,1)S(1)}, bf16[8,2,512,128]{3,2,1,0:T(8,128)(2,1)}, u32[]{:S(2)}) copy-start(bf16[8,2,512,128]{3,2,1,0:T(8,128)(2,1)} %param.32) | copy-start | bytes 6291460
  7.2 5.6 copy-start.12
  7.2 5.6 copy-start.67
  7.2 5.6 copy-start.44
  7.2 71.3 %all-reduce.8.cloned.1.call-start = ((), (), s32[]{:S(2)}) async-start(), calls=%async_computation.3 | async-start | bytes 4194304 | tf_op jit(solution)/shard_map/psum | solution.py:181
  9.0 4.4 copy-start.65
  9.3 4.8 copy-start.22
  9.3 4.8 copy-start.24
  10.2 3.2 copy-start.31
  14.1 4.8 copy-start.46
  14.1 4.8 copy-start.48
  14.2 4.7 copy-start.33
  14.2 4.7 copy-start.35
  18.9 2.8 copy-start.70
  19.0 3.5 copy-start.20
  24.3 1410.0 %all-reduce.10.cloned.1.call-start = ((), (), s32[]{:S(2)}) async-start(), calls=%async_computation.4 | async-start | bytes 4194304 | tf_op jit(solution)/shard_map/psum | solution.py:224
  76.2 54.0 %copy-start.51 = (pred[32,192]{1,0:T(8,128)(4,1)}, pred[32,192]{1,0:T(8,128)(4,1)S(1)}, u32[]{:S(2)}) copy-start(pred[32,192]{1,0:T(8,128)(4,1)S(1)} %broadcast_in_dim.71) | copy-start | bytes 18436
  76.3 5.6 copy-start.55
  80.6 28.3 %copy-start.59 = (f32[512]{0:T(512)}, f32[512]{0:T(512)S(1)}, u32[]{:S(2)}) copy-start(f32[512]{0:T(512)S(1)} %add_rsqrt_fusion) | copy-start | bytes 6148
  82.1 997.5 %copy-start.1 = (bf16[512,1024]{1,0:T(8,128)(2,1)}, bf16[512,1024]{1,0:T(8,128)(2,1)S(1)}, u32[]{:S(2)}) copy-start(bf16[512,1024]{1,0:T(8,128)(2,1)S(1)} %multiply_convert_fusion.5) | copy-start | bytes 3145732
  434.4 541.3 %collective-permute-start = (f32[8,1536,2,128]{3,1,2,0:T(8,128)}, f32[8,1536,2,128]{3,1,2,0:T(8,128)}, u32[]{:S(2)}, u32[]{:S(2)}) collective-permute-start(f32[8,1536,2,128]{3,1,2,0:T(8,128)} %fusion.83), channel_id=1, source_target_pairs={{0,16},{4,20},{8,24},{12,28},{16,0},{20,4},{24,8},{28,12},{1,17},{... | collective-permute-start | bytes 37748744 | tf_op jit(solution)/shard_map/ppermute | solution.py:51
  984.7 4.5 copy-start.5
  990.9 6.3 copy-start.10
  997.2 82.4 %copy-start.41 = (bf16[1024,32]{0,1:T(8,128)(2,1)S(1)}, bf16[1024,32]{0,1:T(8,128)(2,1)}, u32[]{:S(2)}) copy-start(bf16[1024,32]{0,1:T(8,128)(2,1)} %param.31) | copy-start | bytes 196612
  1005.7 39.5 %collective-permute-start.2 = (bf16[1,8,1,192,512]{4,3,1,0,2:T(8,128)(2,1)}, bf16[1,8,1,192,512]{4,3,1,0,2:T(8,128)(2,1)}, u32[]{:S(2)}, u32[]{:S(2)}) collective-permute-start(bf16[1,8,1,192,512]{4,3,1,0,2:T(8,128)(2,1)} %get-tuple-element.124), channel_id=1, source_target_pairs={{0,8},{4,12},{8,16},{12,20},{16,24},{20,28},{24,0},{28,4},{1,9},{5... | collective-permute-start | bytes 4718600 | tf_op jit(solution)/shard_map/ppermute | solution.py:38
  1005.7 73.6 %collective-permute-start.1 = (bf16[1,8,1,192,512]{4,3,1,0,2:T(8,128)(2,1)}, bf16[1,8,1,192,512]{4,3,1,0,2:T(8,128)(2,1)}, u32[]{:S(2)}, u32[]{:S(2)}) collective-permute-start(bf16[1,8,1,192,512]{4,3,1,0,2:T(8,128)(2,1)} %get-tuple-element.125), channel_id=1, source_target_pairs={{0,4},{4,8},{8,12},{12,16},{16,20},{20,24},{24,28},{28,0},{1,5},{5... | collective-permute-start | bytes 4718600 | tf_op jit(solution)/shard_map/ppermute | solution.py:38
  1006.6 172.8 %collective-permute-start.3 = (bf16[1,8,1,192,512]{4,3,1,0,2:T(8,128)(2,1)}, bf16[1,8,1,192,512]{4,3,1,0,2:T(8,128)(2,1)}, u32[]{:S(2)}, u32[]{:S(2)}) collective-permute-start(bf16[1,8,1,192,512]{4,3,1,0,2:T(8,128)(2,1)} %get-tuple-element.123), channel_id=1, source_target_pairs={{0,12},{4,16},{8,20},{12,24},{16,28},{20,0},{24,4},{28,8},{1,13},{... | collective-permute-start | bytes 4718600 | tf_op jit(solution)/shard_map/ppermute | solution.py:38
  1009.5 171.5 %collective-permute-start.4 = (bf16[1,8,1,192,512]{4,3,1,0,2:T(8,128)(2,1)}, bf16[1,8,1,192,512]{4,3,1,0,2:T(8,128)(2,1)}, u32[]{:S(2)}, u32[]{:S(2)}) collective-permute-start(bf16[1,8,1,192,512]{4,3,1,0,2:T(8,128)(2,1)} %get-tuple-element.122), channel_id=1, source_target_pairs={{0,16},{4,20},{8,24},{12,28},{16,0},{20,4},{24,8},{28,12},{1,17},{... | collective-permute-start | bytes 4718600 | tf_op jit(solution)/shard_map/ppermute | solution.py:38
  1011.0 171.7 %collective-permute-start.5 = (bf16[1,8,1,192,512]{4,3,1,0,2:T(8,128)(2,1)}, bf16[1,8,1,192,512]{4,3,1,0,2:T(8,128)(2,1)}, u32[]{:S(2)}, u32[]{:S(2)}) collective-permute-start(bf16[1,8,1,192,512]{4,3,1,0,2:T(8,128)(2,1)} %get-tuple-element.121), channel_id=1, source_target_pairs={{0,20},{4,24},{8,28},{12,0},{16,4},{20,8},{24,12},{28,16},{1,21},{... | collective-permute-start | bytes 4718600 | tf_op jit(solution)/shard_map/ppermute | solution.py:38
  1045.1 139.1 %collective-permute-start.6 = (bf16[1,8,1,192,512]{4,3,1,0,2:T(8,128)(2,1)}, bf16[1,8,1,192,512]{4,3,1,0,2:T(8,128)(2,1)}, u32[]{:S(2)}, u32[]{:S(2)}) collective-permute-start(bf16[1,8,1,192,512]{4,3,1,0,2:T(8,128)(2,1)} %get-tuple-element.120), channel_id=1, source_target_pairs={{0,24},{4,28},{8,0},{12,4},{16,8},{20,12},{24,16},{28,20},{1,25},{... | collective-permute-start | bytes 4718600 | tf_op jit(solution)/shard_map/ppermute | solution.py:38
  1079.3 129.4 %collective-permute-start.7 = (bf16[1,8,1,192,512]{4,3,1,0,2:T(8,128)(2,1)}, bf16[1,8,1,192,512]{4,3,1,0,2:T(8,128)(2,1)}, u32[]{:S(2)}, u32[]{:S(2)}) collective-permute-start(bf16[1,8,1,192,512]{4,3,1,0,2:T(8,128)(2,1)} %get-tuple-element.119), channel_id=1, source_target_pairs={{0,28},{4,0},{8,4},{12,8},{16,12},{20,16},{24,20},{28,24},{1,29},{... | collective-permute-start | bytes 4718600 | tf_op jit(solution)/shard_map/ppermute | solution.py:38
  1080.1 6.6 copy-start.29
  1080.2 6.5 copy-start.53
  1080.2 6.5 copy-start.57
  1304.1 1208.5 %all-reduce.12.cloned.1.call-start = ((), (), s32[]{:S(2)}) async-start(), calls=%async_computation.5 | async-start | bytes 4194304 | tf_op jit(solution)/shard_map/psum | solution.py:266
  1399.8 34.5 %copy-start.61 = (f32[512]{0:T(512)}, f32[512]{0:T(512)S(1)}, u32[]{:S(2)}) copy-start(f32[512]{0:T(512)S(1)} %convert_multiply_fusion.3) | copy-start | bytes 6148
  1437.3 26.8 copy-start.3
  1464.1 31.3 %copy-start.52 = (pred[32,192]{1,0:T(8,128)(4,1)S(1)}, pred[32,192]{1,0:T(8,128)(4,1)}, u32[]{:S(2)}) copy-start(pred[32,192]{1,0:T(8,128)(4,1)} %copy-done.51) | copy-start | bytes 18436
  1782.2 6.5 copy-start.4
  1788.7 270.7 %collective-permute-start.8 = (f32[8,1536,128]{2,1,0:T(8,128)}, f32[8,1536,128]{2,1,0:T(8,128)}, u32[]{:S(2)}, u32[]{:S(2)}) collective-permute-start(f32[8,1536,128]{2,1,0:T(8,128)} %fusion.84), channel_id=1, source_target_pairs={{0,16},{4,20},{8,24},{12,28},{16,0},{20,4},{24,8},{28,12},{1,17},{... | collective-permute-start | bytes 18874376 | tf_op jit(solution)/shard_map/ppermute | solution.py:51
  2462.0 105.3 %all-reduce.14.cloned.1.call-start = ((), (), s32[]{:S(2)}) async-start(), calls=%async_computation.6 | async-start | bytes 2097152 | tf_op jit(solution)/shard_map/psum | solution.py:344
  2462.2 20.3 copy-start.30
  2462.3 20.3 copy-start.54
  2462.3 20.3 copy-start.58
  2462.3 20.3 copy-start.40
  2462.3 20.4 copy-start.2
  2462.3 50.3 %copy-start.42 = (bf16[1024,32]{0,1:T(8,128)(2,1)S(1)}, bf16[1024,32]{0,1:T(8,128)(2,1)}, u32[]{:S(2)}) copy-start(bf16[1024,32]{0,1:T(8,128)(2,1)} %param.31) | copy-start | bytes 196612
  2462.3 50.3 %copy-start.56 = (f32[1024]{0:T(1024)S(1)}, f32[1024]{0:T(1024)}, u32[]{:S(2)}) copy-start(f32[1024]{0:T(1024)} %param.30) | copy-start | bytes 12292
  2462.3 50.3 %copy-start.60 = (f32[512]{0:T(512)S(1)}, f32[512]{0:T(512)}, u32[]{:S(2)}) copy-start(f32[512]{0:T(512)} %copy-done.59) | copy-start | bytes 6148
  2483.7 34.0 %copy-start.14 = (bf16[512,1024]{1,0:T(8,128)(2,1)S(1)}, bf16[512,1024]{1,0:T(8,128)(2,1)}, u32[]{:S(2)}) copy-start(bf16[512,1024]{1,0:T(8,128)(2,1)} %param.22) | copy-start | bytes 3145732
  2483.7 34.0 %copy-start.62 = (f32[512]{0:T(512)S(1)}, f32[512]{0:T(512)}, u32[]{:S(2)}) copy-start(f32[512]{0:T(512)} %copy-done.61) | copy-start | bytes 6148
  2512.7 5.0 copy-start.7
  2512.7 5.0 copy-start.11
  2517.7 2.7 copy-start.17
  2530.8 175.2 %all-reduce.16.cloned.1.call-start = ((), (), s32[]{:S(2)}) async-start(), calls=%async_computation.7 | async-start | bytes 6553600 | tf_op jit(solution)/shard_map/psum | solution.py:350
  2534.8 9.2 copy-start.18
  2534.8 9.2 copy-start.19
  2554.1 5.4 copy-start.64
  2554.1 5.4 copy-start.72
  2559.5 9.8 copy-start.69
  2706.0 2.4 copy-start.38
  2706.0 3.2 copy-start.37
  2706.0 4.0 copy-start.26
  2708.5 2.6 copy-start.50
  (24 other events, 33.9 us)
Sparse Core Ops, SparseCore 0:
  24.4 54.0 all-reduce.7
  1304.2 123.0 all-reduce.9
  2462.1 50.4 all-reduce.11
  2530.9 36.3 all-reduce.13
  2572.0 134.0 all-reduce.15
